TPU v7x, 256 devices: a whole 4x4x8 slice. The times are simulated.
256 devices in a mesh: seq: 16 (over z, core), rep: 16 (over x, y).
Axes of the slice: x: 4, y: 4, z: 8, core: 2. Of those that a mesh axis runs over, the one named last changes fastest.
Arguments:
- tokens: bfloat16 [65536, 1024], P(('rep', 'seq')), parts along dimension 0, may hold values from -16 to 16
- segments: int32 [65536], P(('rep', 'seq')), parts along dimension 0, may hold values from 0 to 3, never falling along the last dimension, each value on 1 to 2048 neighbouring positions
- qkv_weight: bfloat16 [1024, 3072], replicated, may hold values from -1 to 1
- out_weight: bfloat16 [1024, 1024], replicated, may hold values from -0.1875 to 0.1875
- out_bias: float32 [1024], replicated, may hold values from -3 to 3
- ln_gain: float32 [1024], replicated, may hold values from 0.1 to 1.9
- ln_bias: float32 [1024], replicated, may hold values from -3 to 3
Outputs:
- normed: bfloat16 [65536, 1024], P(('rep', 'seq')), parts along dimension 0
- kv_cache: bfloat16 [65536, 2048], P('rep', 'seq'), parts along dimension 0
There are 16 independent parts, one for each index of `rep`. A program takes and returns all parts, laid end to end along the dimension named above; an argument that names none is the same for every part. Nothing has to cross between parts.
Inputs may be any that keep to these rules, and one draw needn't show every extreme that they name: `segments`: each prompt is a contiguous run of 1 to 2048 tokens, numbers never falling, one prompt exactly 2048 tokens.
All inputs are finite; a program needn't handle non-finite values.
Results may differ from a plain program's by a relative error of at most 0.008.
Values may be sent and summed in bfloat16 or wider, within the bound.
A program may use at most 128 MiB of HBM per device.

v0:
```python
import math
import jax
import jax.numpy as jnp
from jax import lax
from jax.sharding import PartitionSpec as P

HEADS = 16
HEAD = 64
Q_CHUNK = 512


def shards(tokens, segments, qkv_weight, out_weight, out_bias, ln_gain, ln_bias):
    tok_rows, width = tokens.shape
    scale = 1.0 / math.sqrt(HEAD)
    all_seg = lax.all_gather(segments, "seq", axis=0, tiled=True)
    proj = jnp.dot(tokens, qkv_weight, preferred_element_type=jnp.float32).astype(jnp.bfloat16)
    grouped = proj.reshape(tok_rows, HEADS, 3 * HEAD)
    mine = lax.all_to_all(grouped, "seq", split_axis=1, concat_axis=0, tiled=True)
    count_rows = mine.shape[0]
    mine = mine.reshape(count_rows, 3 * HEAD)
    kv_cache = mine[:, HEAD:]
    query = mine[:, :HEAD]
    key_h = mine[:, HEAD : 2 * HEAD]
    value_h = mine[:, 2 * HEAD :]
    chunks = count_rows // Q_CHUNK

    def per_chunk(items):
        q_c, seg_c = items
        kept = seg_c[:, None] == all_seg[None, :]
        score = jnp.dot(q_c, key_h.T, preferred_element_type=jnp.float32) * scale
        score = jnp.where(kept, score, -1e30)
        top = jnp.max(score, axis=1, keepdims=True)
        weight = jnp.where(kept, jnp.exp(score - top), 0.0)
        total = jnp.sum(weight, axis=1, keepdims=True)
        acc = jnp.dot(weight.astype(jnp.bfloat16), value_h, preferred_element_type=jnp.float32)
        return (acc / total).astype(jnp.bfloat16)

    context = lax.map(
        per_chunk, (query.reshape(chunks, Q_CHUNK, HEAD), all_seg.reshape(chunks, Q_CHUNK))
    ).reshape(count_rows, 1, HEAD)
    gathered_ctx = lax.all_to_all(context, "seq", split_axis=0, concat_axis=1, tiled=True)
    gathered_ctx = gathered_ctx.reshape(tok_rows, width)
    mixed = (
        jnp.dot(gathered_ctx, out_weight, preferred_element_type=jnp.float32)
        + out_bias
        + tokens.astype(jnp.float32)
    )
    mean = jnp.mean(mixed, axis=1, keepdims=True)
    centered = mixed - mean
    variance = jnp.mean(centered * centered, axis=1, keepdims=True)
    normed = centered / jnp.sqrt(variance + 1e-05) * ln_gain + ln_bias
    return (normed.astype(jnp.bfloat16), kv_cache)


def solution(mesh):
    in_specs = (P(("rep", "seq"), None), P(("rep", "seq")), P(), P(), P(), P(), P())
    out_specs = (P(("rep", "seq"), None), P("rep", "seq"))
    return jax.shard_map(shards, mesh=mesh, in_specs=in_specs, out_specs=out_specs, check_vma=False)
```

profile of v0, /device:TPU:1, one launch (start us, length us, event | category | flops | bytes accessed | tf_op | source)
XLA Modules:
  0.0 213.7 jit_solution(3142455166517597984)
XLA Ops:
  0.7 6.0 %convolution_convert_fusion = bf16[256,3072]{1,0:T(8,128)(2,1)} fusion(bf16[256,1024]{1,0:T(8,128)(2,1)} %param.9, bf16[1024,3072]{1,0:T(8,128)(2,1)} %param.11), kind=kOutput, calls=%fused_computation.18 | convolution fusion | flops 1611399168 | bytes 8388608 | tf_op jit(solution)/shard_map/dot_general | solution.py:16
  9.3 10.0 %all-to-all-start = ((bf16[256,16,192]{0,2,1:T(8,128)(2,1)}), bf16[256,16,192]{0,2,1:T(8,128)(2,1)}, u32[]{:S(2)}, u32[]{:S(2)}) async-start(bf16[256,16,192]{0,2,1:T(8,128)(2,1)} %bitcast.51), calls=%async_computation | async-start | bytes 3145728 | tf_op jit(solution)/shard_map/all_to_all | solution.py:18
  19.3 48.2 %all-gather = s32[16,1,256]{2,1,0:T(1,128)S(1)} all-gather(s32[1,1,256]{2,1,0:T(1,128)S(1)} %bitcast.60), channel_id=1, replica_groups=mesh['seq'=16,'rep'=16] {'seq'}, dimensions={0}, use_global_device_ids=true | all-gather | bytes 17408 | tf_op jit(solution)/shard_map/all_gather | solution.py:15
  76.2 70.4 %while.10 = (s32[]{:T(128)}, bf16[8,512,64]{1,2,0:T(8,128)(2,1)}, s32[8,512]{1,0:T(8,128)S(1)}, s32[4096]{0:T(1024)S(1)}, bf16[8,512,64]{2,1,0:T(8,128)(2,1)}, /...) while((s32[]{:T(128)}, bf16[8,512,64]{1,2,0:T(8,128)(2,1)}, s32[8,512]{1,0:T(8,128)S(1)}, ...), condition=%wide.region_3.4_spmd, body=%wide.region_0.3_spmd.sunk | while | flops 570489856 | bytes 29102212 | solution.py:38
  76.3 2.9 %fusion.42 = (f32[512]{0:T(512)S(1)}, f32[512,4096]{1,0:T(8,128)S(1)}) fusion(s32[4096]{0:T(1024)S(1)} %get-tuple-element.145, s32[512]{0:T(512)S(1)} %bitcast.57, bf16[4096,64]{1,0:T(8,128)(2,1)} %get-tuple-element.147, bf16[8,512,64]{2,1,0:T(8,128)(2,1)} %get-tuple-element.146, s32[]{:T(128)S(6)} %copy.40), kind=kOutput, calls=%fused_computation.2.clone.1 | convolution fusion | flops 276823552 | bytes 9588740 | tf_op jit(solution)/shard_map/while/body/eval_jaxpr/dot_general | solution.py:30
  81.8 3.3 %fusion.44 = bf16[8,512,64]{1,2,0:T(8,128)(2,1)} fusion(bf16[8,512,64]{1,2,0:T(8,128)(2,1)} %get-tuple-element.135, s32[]{:T(128)S(6)} %copy.40, bf16[4096,64]{1,0:T(8,128)(2,1)S(1)} %copy-done.2, f32[512,4096]{1,0:T(8,128)S(1)} %get-tuple-element.124, f32[512]{0:T(512)S(1)} %get-tuple-element.125, s32[4096]{0:T(1024)S(1)} %get-tuple-element.145, ...), kind=kOutput, calls=%fused_computation.9.clone.1 | convolution fusion | flops 281083904 | bytes 9000964 | tf_op jit(solution)/shard_map/while/body/eval_jaxpr/dot_general | solution.py:35
  85.1 2.9 %fusion.42 = (f32[512]{0:T(512)S(1)}, f32[512,4096]{1,0:T(8,128)S(1)}) fusion(s32[4096]{0:T(1024)S(1)} %get-tuple-element.145, s32[512]{0:T(512)S(1)} %bitcast.57, bf16[4096,64]{1,0:T(8,128)(2,1)} %get-tuple-element.147, bf16[8,512,64]{2,1,0:T(8,128)(2,1)} %get-tuple-element.146, s32[]{:T(128)S(6)} %copy.40), kind=kOutput, calls=%fused_computation.2.clone.1 | convolution fusion | flops 276823552 | bytes 9588740 | tf_op jit(solution)/shard_map/while/body/eval_jaxpr/dot_general | solution.py:30
  90.6 3.3 %fusion.44 = bf16[8,512,64]{1,2,0:T(8,128)(2,1)} fusion(bf16[8,512,64]{1,2,0:T(8,128)(2,1)} %get-tuple-element.135, s32[]{:T(128)S(6)} %copy.40, bf16[4096,64]{1,0:T(8,128)(2,1)S(1)} %copy-done.2, f32[512,4096]{1,0:T(8,128)S(1)} %get-tuple-element.124, f32[512]{0:T(512)S(1)} %get-tuple-element.125, s32[4096]{0:T(1024)S(1)} %get-tuple-element.145, ...), kind=kOutput, calls=%fused_computation.9.clone.1 | convolution fusion | flops 281083904 | bytes 9000964 | tf_op jit(solution)/shard_map/while/body/eval_jaxpr/dot_general | solution.py:35
  93.9 2.9 %fusion.42 = (f32[512]{0:T(512)S(1)}, f32[512,4096]{1,0:T(8,128)S(1)}) fusion(s32[4096]{0:T(1024)S(1)} %get-tuple-element.145, s32[512]{0:T(512)S(1)} %bitcast.57, bf16[4096,64]{1,0:T(8,128)(2,1)} %get-tuple-element.147, bf16[8,512,64]{2,1,0:T(8,128)(2,1)} %get-tuple-element.146, s32[]{:T(128)S(6)} %copy.40), kind=kOutput, calls=%fused_computation.2.clone.1 | convolution fusion | flops 276823552 | bytes 9588740 | tf_op jit(solution)/shard_map/while/body/eval_jaxpr/dot_general | solution.py:30
  99.4 3.3 %fusion.44 = bf16[8,512,64]{1,2,0:T(8,128)(2,1)} fusion(bf16[8,512,64]{1,2,0:T(8,128)(2,1)} %get-tuple-element.135, s32[]{:T(128)S(6)} %copy.40, bf16[4096,64]{1,0:T(8,128)(2,1)S(1)} %copy-done.2, f32[512,4096]{1,0:T(8,128)S(1)} %get-tuple-element.124, f32[512]{0:T(512)S(1)} %get-tuple-element.125, s32[4096]{0:T(1024)S(1)} %get-tuple-element.145, ...), kind=kOutput, calls=%fused_computation.9.clone.1 | convolution fusion | flops 281083904 | bytes 9000964 | tf_op jit(solution)/shard_map/while/body/eval_jaxpr/dot_general | solution.py:35
  102.7 2.9 %fusion.42 = (f32[512]{0:T(512)S(1)}, f32[512,4096]{1,0:T(8,128)S(1)}) fusion(s32[4096]{0:T(1024)S(1)} %get-tuple-element.145, s32[512]{0:T(512)S(1)} %bitcast.57, bf16[4096,64]{1,0:T(8,128)(2,1)} %get-tuple-element.147, bf16[8,512,64]{2,1,0:T(8,128)(2,1)} %get-tuple-element.146, s32[]{:T(128)S(6)} %copy.40), kind=kOutput, calls=%fused_computation.2.clone.1 | convolution fusion | flops 276823552 | bytes 9588740 | tf_op jit(solution)/shard_map/while/body/eval_jaxpr/dot_general | solution.py:30
  108.2 3.3 %fusion.44 = bf16[8,512,64]{1,2,0:T(8,128)(2,1)} fusion(bf16[8,512,64]{1,2,0:T(8,128)(2,1)} %get-tuple-element.135, s32[]{:T(128)S(6)} %copy.40, bf16[4096,64]{1,0:T(8,128)(2,1)S(1)} %copy-done.2, f32[512,4096]{1,0:T(8,128)S(1)} %get-tuple-element.124, f32[512]{0:T(512)S(1)} %get-tuple-element.125, s32[4096]{0:T(1024)S(1)} %get-tuple-element.145, ...), kind=kOutput, calls=%fused_computation.9.clone.1 | convolution fusion | flops 281083904 | bytes 9000964 | tf_op jit(solution)/shard_map/while/body/eval_jaxpr/dot_general | solution.py:35
  117.0 3.3 %fusion.44 = bf16[8,512,64]{1,2,0:T(8,128)(2,1)} fusion(bf16[8,512,64]{1,2,0:T(8,128)(2,1)} %get-tuple-element.135, s32[]{:T(128)S(6)} %copy.40, bf16[4096,64]{1,0:T(8,128)(2,1)S(1)} %copy-done.2, f32[512,4096]{1,0:T(8,128)S(1)} %get-tuple-element.124, f32[512]{0:T(512)S(1)} %get-tuple-element.125, s32[4096]{0:T(1024)S(1)} %get-tuple-element.145, ...), kind=kOutput, calls=%fused_computation.9.clone.1 | convolution fusion | flops 281083904 | bytes 9000964 | tf_op jit(solution)/shard_map/while/body/eval_jaxpr/dot_general | solution.py:35
  120.3 2.9 %fusion.42 = (f32[512]{0:T(512)S(1)}, f32[512,4096]{1,0:T(8,128)S(1)}) fusion(s32[4096]{0:T(1024)S(1)} %get-tuple-element.145, s32[512]{0:T(512)S(1)} %bitcast.57, bf16[4096,64]{1,0:T(8,128)(2,1)} %get-tuple-element.147, bf16[8,512,64]{2,1,0:T(8,128)(2,1)} %get-tuple-element.146, s32[]{:T(128)S(6)} %copy.40), kind=kOutput, calls=%fused_computation.2.clone.1 | convolution fusion | flops 276823552 | bytes 9588740 | tf_op jit(solution)/shard_map/while/body/eval_jaxpr/dot_general | solution.py:30
  125.8 3.3 %fusion.44 = bf16[8,512,64]{1,2,0:T(8,128)(2,1)} fusion(bf16[8,512,64]{1,2,0:T(8,128)(2,1)} %get-tuple-element.135, s32[]{:T(128)S(6)} %copy.40, bf16[4096,64]{1,0:T(8,128)(2,1)S(1)} %copy-done.2, f32[512,4096]{1,0:T(8,128)S(1)} %get-tuple-element.124, f32[512]{0:T(512)S(1)} %get-tuple-element.125, s32[4096]{0:T(1024)S(1)} %get-tuple-element.145, ...), kind=kOutput, calls=%fused_computation.9.clone.1 | convolution fusion | flops 281083904 | bytes 9000964 | tf_op jit(solution)/shard_map/while/body/eval_jaxpr/dot_general | solution.py:35
  134.6 3.3 %fusion.44 = bf16[8,512,64]{1,2,0:T(8,128)(2,1)} fusion(bf16[8,512,64]{1,2,0:T(8,128)(2,1)} %get-tuple-element.135, s32[]{:T(128)S(6)} %copy.40, bf16[4096,64]{1,0:T(8,128)(2,1)S(1)} %copy-done.2, f32[512,4096]{1,0:T(8,128)S(1)} %get-tuple-element.124, f32[512]{0:T(512)S(1)} %get-tuple-element.125, s32[4096]{0:T(1024)S(1)} %get-tuple-element.145, ...), kind=kOutput, calls=%fused_computation.9.clone.1 | convolution fusion | flops 281083904 | bytes 9000964 | tf_op jit(solution)/shard_map/while/body/eval_jaxpr/dot_general | solution.py:35
  137.9 2.9 %fusion.42 = (f32[512]{0:T(512)S(1)}, f32[512,4096]{1,0:T(8,128)S(1)}) fusion(s32[4096]{0:T(1024)S(1)} %get-tuple-element.145, s32[512]{0:T(512)S(1)} %bitcast.57, bf16[4096,64]{1,0:T(8,128)(2,1)} %get-tuple-element.147, bf16[8,512,64]{2,1,0:T(8,128)(2,1)} %get-tuple-element.146, s32[]{:T(128)S(6)} %copy.40), kind=kOutput, calls=%fused_computation.2.clone.1 | convolution fusion | flops 276823552 | bytes 9588740 | tf_op jit(solution)/shard_map/while/body/eval_jaxpr/dot_general | solution.py:30
  143.4 3.3 %fusion.44 = bf16[8,512,64]{1,2,0:T(8,128)(2,1)} fusion(bf16[8,512,64]{1,2,0:T(8,128)(2,1)} %get-tuple-element.135, s32[]{:T(128)S(6)} %copy.40, bf16[4096,64]{1,0:T(8,128)(2,1)S(1)} %copy-done.2, f32[512,4096]{1,0:T(8,128)S(1)} %get-tuple-element.124, f32[512]{0:T(512)S(1)} %get-tuple-element.125, s32[4096]{0:T(1024)S(1)} %get-tuple-element.145, ...), kind=kOutput, calls=%fused_computation.9.clone.1 | convolution fusion | flops 281083904 | bytes 9000964 | tf_op jit(solution)/shard_map/while/body/eval_jaxpr/dot_general | solution.py:35
  148.2 3.2 %reshape.53 = bf16[4096,1,64]{2,1,0:T(2,128)(2,1)} reshape(bf16[8,512,64]{2,1,0:T(8,128)(2,1)S(1)} %copy.32) | data formatting | bytes 1048576 | tf_op jit(solution)/shard_map/reshape | solution.py:40
  151.9 23.5 %reduce.1 = bf16[4096,64]{1,0:T(8,128)(2,1)S(1)} reduce(bf16[4096,1,64]{2,1,0:T(2,128)(2,1)} %reshape.53, bf16[]{:T(256)} %broadcast.45), dimensions={1}, to_apply=%reshape.53.reduce_sub_computation | reduce | bytes 1048578 | tf_op jit(solution)/shard_map/reshape | solution.py:40
  176.8 5.9 %all-to-all-start.1 = ((bf16[16,2,8192]{2,1,0:T(2,128)(2,1)}), bf16[16,2,8192]{2,1,0:T(2,128)(2,1)}, u32[]{:S(2)}, u32[]{:S(2)}) async-start(bf16[16,2,8192]{2,1,0:T(2,128)(2,1)} %reshape.55), calls=%async_computation.1 | async-start | bytes 1048576 | tf_op jit(solution)/shard_map/all_to_all | solution.py:41
  185.4 14.7 %all-to-all-done.1 = bf16[16,2,8192]{2,1,0:T(2,128)(2,1)} async-done(((bf16[16,2,8192]{2,1,0:T(2,128)(2,1)}), bf16[16,2,8192]{2,1,0:T(2,128)(2,1)}, u32[]{:S(2)}, u32[]{:S(2)}) %all-to-all-start.1) | async-done | bytes 524320 | tf_op jit(solution)/shard_map/all_to_all | solution.py:41
  200.1 5.5 %reshape.56 = bf16[4096,1,64]{2,1,0:T(2,128)(2,1)} reshape(bf16[16,2,8192]{2,1,0:T(2,128)(2,1)} %all-to-all-done.1) | data formatting | bytes 1048576
  205.6 4.6 %copy.28 = bf16[4096,1,64]{0,2,1:T(8,128)(2,1)S(1)} copy(bf16[4096,1,64]{2,1,0:T(2,128)(2,1)} %reshape.56) | data formatting | bytes 1048576 | tf_op jit(solution)/shard_map/all_to_all | solution.py:41
  (68 shorter events, 47.8 us)
Async XLA Ops:
  0.6 209.9 %copy-start = (bf16[1024,1024]{1,0:T(8,128)(2,1)S(1)}, bf16[1024,1024]{1,0:T(8,128)(2,1)}, u32[]{:S(2)}) copy-start(bf16[1024,1024]{1,0:T(8,128)(2,1)} %param.12) | copy-start | bytes 6291460
  0.6 18.6 %copy-start.6 = (s32[256]{0:T(256)S(1)}, s32[256]{0:T(256)}, u32[]{:S(2)}) copy-start(s32[256]{0:T(256)} %param.10) | copy-start | bytes 3076
  9.3 58.2 %all-to-all-start = ((bf16[256,16,192]{0,2,1:T(8,128)(2,1)}), bf16[256,16,192]{0,2,1:T(8,128)(2,1)}, u32[]{:S(2)}, u32[]{:S(2)}) async-start(bf16[256,16,192]{0,2,1:T(8,128)(2,1)} %bitcast.51), calls=%async_computation | async-start | bytes 3145728 | tf_op jit(solution)/shard_map/all_to_all | solution.py:18
  69.1 1.2 copy-start.1
  76.2 5.5 %copy-start.2 = (bf16[4096,64]{1,0:T(8,128)(2,1)S(1)}, bf16[4096,64]{1,0:T(8,128)(2,1)}, u32[]{:S(2)}) copy-start(bf16[4096,64]{1,0:T(8,128)(2,1)} %get-tuple-element.148) | copy-start | bytes 1572868 | tf_op jit(solution)/shard_map/while
  85.1 5.5 %copy-start.2 = (bf16[4096,64]{1,0:T(8,128)(2,1)S(1)}, bf16[4096,64]{1,0:T(8,128)(2,1)}, u32[]{:S(2)}) copy-start(bf16[4096,64]{1,0:T(8,128)(2,1)} %get-tuple-element.148) | copy-start | bytes 1572868 | tf_op jit(solution)/shard_map/while
  93.9 5.5 %copy-start.2 = (bf16[4096,64]{1,0:T(8,128)(2,1)S(1)}, bf16[4096,64]{1,0:T(8,128)(2,1)}, u32[]{:S(2)}) copy-start(bf16[4096,64]{1,0:T(8,128)(2,1)} %get-tuple-element.148) | copy-start | bytes 1572868 | tf_op jit(solution)/shard_map/while
  102.7 5.5 %copy-start.2 = (bf16[4096,64]{1,0:T(8,128)(2,1)S(1)}, bf16[4096,64]{1,0:T(8,128)(2,1)}, u32[]{:S(2)}) copy-start(bf16[4096,64]{1,0:T(8,128)(2,1)} %get-tuple-element.148) | copy-start | bytes 1572868 | tf_op jit(solution)/shard_map/while
  111.5 5.5 %copy-start.2 = (bf16[4096,64]{1,0:T(8,128)(2,1)S(1)}, bf16[4096,64]{1,0:T(8,128)(2,1)}, u32[]{:S(2)}) copy-start(bf16[4096,64]{1,0:T(8,128)(2,1)} %get-tuple-element.148) | copy-start | bytes 1572868 | tf_op jit(solution)/shard_map/while
  120.3 5.5 %copy-start.2 = (bf16[4096,64]{1,0:T(8,128)(2,1)S(1)}, bf16[4096,64]{1,0:T(8,128)(2,1)}, u32[]{:S(2)}) copy-start(bf16[4096,64]{1,0:T(8,128)(2,1)} %get-tuple-element.148) | copy-start | bytes 1572868 | tf_op jit(solution)/shard_map/while
  129.1 5.5 %copy-start.2 = (bf16[4096,64]{1,0:T(8,128)(2,1)S(1)}, bf16[4096,64]{1,0:T(8,128)(2,1)}, u32[]{:S(2)}) copy-start(bf16[4096,64]{1,0:T(8,128)(2,1)} %get-tuple-element.148) | copy-start | bytes 1572868 | tf_op jit(solution)/shard_map/while
  137.9 5.5 %copy-start.2 = (bf16[4096,64]{1,0:T(8,128)(2,1)S(1)}, bf16[4096,64]{1,0:T(8,128)(2,1)}, u32[]{:S(2)}) copy-start(bf16[4096,64]{1,0:T(8,128)(2,1)} %get-tuple-element.148) | copy-start | bytes 1572868 | tf_op jit(solution)/shard_map/while
  151.9 58.6 %copy-start.3 = (f32[1024]{0:T(1024)S(1)}, f32[1024]{0:T(1024)}, u32[]{:S(2)}) copy-start(f32[1024]{0:T(1024)} %param.13) | copy-start | bytes 12292
  176.8 23.2 %all-to-all-start.1 = ((bf16[16,2,8192]{2,1,0:T(2,128)(2,1)}), bf16[16,2,8192]{2,1,0:T(2,128)(2,1)}, u32[]{:S(2)}, u32[]{:S(2)}) async-start(bf16[16,2,8192]{2,1,0:T(2,128)(2,1)} %reshape.55), calls=%async_computation.1 | async-start | bytes 1048576 | tf_op jit(solution)/shard_map/all_to_all | solution.py:41
  182.8 29.9 %copy-start.4 = (f32[1024]{0:T(1024)S(1)}, f32[1024]{0:T(1024)}, u32[]{:S(2)}) copy-start(f32[1024]{0:T(1024)} %param.15) | copy-start | bytes 12292
  182.8 29.9 %copy-start.5 = (f32[1024]{0:T(1024)S(1)}, f32[1024]{0:T(1024)}, u32[]{:S(2)}) copy-start(f32[1024]{0:T(1024)} %param.14) | copy-start | bytes 12292
where the time goes:
time: 215 us; the launch traced here: 214 us
  matrix products  57.2 us (27%)
  blocking collectives  48.2 us (22%)
  other arithmetic  45.8 us (21%)
  local copies, waits for them, and re-layouts  31.1 us (14%)
  starting transfers between devices  15.9 us (7%)
  waiting for transfers between devices  14.7 us (7%)
    all_gather x1, blocking collectives, shards(): all_seg = lax.all_gather(segments, 'seq', axis=0, tiled=True)  48.2 us
    dot_general x8, matrix products, per_chunk(): jnp.dot(weight.astype(jnp.bfloat16), value_h, preferred_element_type=jnp....  26.4 us
    reshape x1, other arithmetic, shards(): context = lax.map(per_chunk, (query.reshape(chunks, Q_CHUNK, HEAD), all_s...  23.5 us
    dot_general x8, matrix products, per_chunk(): score = jnp.dot(q_c, key_h.T, preferred_element_type=jnp.float32) * scale  22.9 us
    reduce_sum x8, other arithmetic, per_chunk(): total = jnp.sum(weight, axis=1, keepdims=True)  21 us
    all_to_all x1, waiting for transfers between devices, shards(): lax.all_to_all(context, 'seq', split_axis=0, concat_axis=1, tiled=True)  14.7 us
    unnamed x17, local copies, waits for them, and re-layouts  11.2 us
    all_to_all x1, starting transfers between devices, shards(): lax.all_to_all(grouped, 'seq', split_axis=1, concat_axis=0, tiled=True)  9.97 us
  transfers between devices with their start and end apart: 2, of which 1 were waited for; matrix products, arithmetic and copies ran while one was open for 1% of the time, Pallas kernels for 0%

commit v1 on v0

--- a/solution.py
+++ b/solution.py
@@ -12,7 +12,8 @@
 def shards(tokens, segments, qkv_weight, out_weight, out_bias, ln_gain, ln_bias):
     tok_rows, width = tokens.shape
     scale = 1.0 / math.sqrt(HEAD)
-    all_seg = lax.all_gather(segments, "seq", axis=0, tiled=True)
+    copies = jnp.concatenate([segments] * lax.axis_size("seq"), axis=0)
+    all_seg = lax.all_to_all(copies, "seq", 0, 0, tiled=True)
     proj = jnp.dot(tokens, qkv_weight, preferred_element_type=jnp.float32).astype(jnp.bfloat16)
     grouped = proj.reshape(tok_rows, HEADS, 3 * HEAD)
     mine = lax.all_to_all(grouped, "seq", split_axis=1, concat_axis=0, tiled=True)

time: 215 us -> 212 us (0.986)
  blocking collectives: 48.2 us -> 0 us
  waiting for transfers between devices: 14.7 us -> 53.2 us
  starting transfers between devices: 15.9 us -> 21.3 us
    all_gather x1 -> x0, blocking collectives: 48.2 us -> none  [shards(): all_seg = lax.all_gather(segments, 'seq', axis=0, tiled=True)]
    all_to_all x1, waiting for transfers between devices: 0.01 us -> 38.6 us  [shards(): lax.all_to_all(grouped, 'seq', split_axis=1, concat_axis=0, tiled=True)]
    all_to_all x0 -> x1, starting transfers between devices: none -> 9.97 us  [shards(): all_seg = lax.all_to_all(copies, 'seq', 0, 0, tiled=True)]
    all_to_all x1, starting transfers between devices: 9.97 us -> 7.23 us  [shards(): lax.all_to_all(grouped, 'seq', split_axis=1, concat_axis=0, tiled=True)]
    unnamed x17 -> x15, local copies, waits for them, and re-layouts: 11.2 us -> 11.2 us
  transfers between devices with their start and end apart: 2 -> 3, of which waited for: 1 -> 2; matrix products, arithmetic and copies ran while one was open for 1% -> 5% of each run, Pallas kernels for 0% -> 0%
where the time goes in v1:
time: 212 us; the launch traced here: 211 us
  matrix products  57.1 us (27%)
  waiting for transfers between devices  53.2 us (25%)
  other arithmetic  45.8 us (22%)
  local copies, waits for them, and re-layouts  32.6 us (15%)
  starting transfers between devices  21.3 us (10%)
    all_to_all x1, waiting for transfers between devices, shards(): lax.all_to_all(grouped, 'seq', split_axis=1, concat_axis=0, tiled=True)  38.6 us
    dot_general x8, matrix products, per_chunk(): jnp.dot(weight.astype(jnp.bfloat16), value_h, preferred_element_type=jnp....  26.4 us
    reshape x1, other arithmetic, shards(): context = lax.map(per_chunk, (query.reshape(chunks, Q_CHUNK, HEAD), all_s...  23.5 us
    dot_general x8, matrix products, per_chunk(): score = jnp.dot(q_c, key_h.T, preferred_element_type=jnp.float32) * scale  22.9 us
    reduce_sum x8, other arithmetic, per_chunk(): total = jnp.sum(weight, axis=1, keepdims=True)  21 us
    all_to_all x1, waiting for transfers between devices, shards(): lax.all_to_all(context, 'seq', split_axis=0, concat_axis=1, tiled=True)  14.7 us
    unnamed x15, local copies, waits for them, and re-layouts  11.2 us
    all_to_all x1, starting transfers between devices, shards(): all_seg = lax.all_to_all(copies, 'seq', 0, 0, tiled=True)  9.97 us
  transfers between devices with their start and end apart: 3, of which 2 were waited for; matrix products, arithmetic and copies ran while one was open for 5% of the time, Pallas kernels for 0%

profile of v1, /device:TPU:1, one launch (start us, length us, event | category | flops | bytes accessed | tf_op | source)
XLA Modules:
  0.0 210.8 jit_solution(17934647127701508251)
XLA Ops:
  2.1 10.0 %all-to-all-start = ((s32[16,256,1]{1,2,0:T(1,128)}), s32[16,256,1]{1,2,0:T(1,128)S(1)}, u32[]{:S(2)}, u32[]{:S(2)}) async-start(s32[16,256,1]{1,2,0:T(1,128)} %concatenate.4), calls=%async_computation | async-start | bytes 32768 | tf_op jit(solution)/shard_map/all_to_all | solution.py:16
  12.1 5.9 %convolution_convert_fusion = bf16[256,3072]{1,0:T(8,128)(2,1)} fusion(bf16[256,1024]{1,0:T(8,128)(2,1)} %param.9, bf16[1024,3072]{1,0:T(8,128)(2,1)} %param.11), kind=kOutput, calls=%fused_computation.18 | convolution fusion | flops 1611399168 | bytes 8388608 | tf_op jit(solution)/shard_map/dot_general | solution.py:17
  20.6 7.2 %all-to-all-start.1 = ((bf16[256,16,192]{0,2,1:T(8,128)(2,1)}), bf16[256,16,192]{0,2,1:T(8,128)(2,1)}, u32[]{:S(2)}, u32[]{:S(2)}) async-start(bf16[256,16,192]{0,2,1:T(8,128)(2,1)} %bitcast.50), calls=%async_computation.1 | async-start | bytes 3145728 | tf_op jit(solution)/shard_map/all_to_all | solution.py:19
  27.9 38.6 %all-to-all-done.1 = bf16[256,16,192]{0,2,1:T(8,128)(2,1)} async-done(((bf16[256,16,192]{0,2,1:T(8,128)(2,1)}), bf16[256,16,192]{0,2,1:T(8,128)(2,1)}, u32[]{:S(2)}, u32[]{:S(2)}) %all-to-all-start.1) | async-done | bytes 1572896 | tf_op jit(solution)/shard_map/all_to_all | solution.py:19
  75.2 70.4 %while.10 = (s32[]{:T(128)}, bf16[8,512,64]{1,2,0:T(8,128)(2,1)}, s32[8,512]{1,0:T(8,128)S(1)}, s32[4096]{0:T(1024)S(1)}, bf16[8,512,64]{2,1,0:T(8,128)(2,1)}, /...) while((s32[]{:T(128)}, bf16[8,512,64]{1,2,0:T(8,128)(2,1)}, s32[8,512]{1,0:T(8,128)S(1)}, ...), condition=%wide.region_3.4_spmd, body=%wide.region_0.3_spmd.sunk | while | flops 570489856 | bytes 29102212 | solution.py:39
  75.2 2.9 %fusion.42 = (f32[512]{0:T(512)S(1)}, f32[512,4096]{1,0:T(8,128)S(1)}) fusion(s32[4096]{0:T(1024)S(1)} %get-tuple-element.145, s32[512]{0:T(512)S(1)} %bitcast.56, bf16[4096,64]{1,0:T(8,128)(2,1)} %get-tuple-element.147, bf16[8,512,64]{2,1,0:T(8,128)(2,1)} %get-tuple-element.146, s32[]{:T(128)S(6)} %copy.40), kind=kOutput, calls=%fused_computation.2.clone.1 | convolution fusion | flops 276823552 | bytes 9588740 | tf_op jit(solution)/shard_map/while/body/eval_jaxpr/dot_general | solution.py:31
  80.7 3.3 %fusion.44 = bf16[8,512,64]{1,2,0:T(8,128)(2,1)} fusion(bf16[8,512,64]{1,2,0:T(8,128)(2,1)} %get-tuple-element.135, s32[]{:T(128)S(6)} %copy.40, bf16[4096,64]{1,0:T(8,128)(2,1)S(1)} %copy-done.2, f32[512,4096]{1,0:T(8,128)S(1)} %get-tuple-element.124, f32[512]{0:T(512)S(1)} %get-tuple-element.125, s32[4096]{0:T(1024)S(1)} %get-tuple-element.145, ...), kind=kOutput, calls=%fused_computation.9.clone.1 | convolution fusion | flops 281083904 | bytes 9000964 | tf_op jit(solution)/shard_map/while/body/eval_jaxpr/dot_general | solution.py:36
  84.0 2.9 %fusion.42 = (f32[512]{0:T(512)S(1)}, f32[512,4096]{1,0:T(8,128)S(1)}) fusion(s32[4096]{0:T(1024)S(1)} %get-tuple-element.145, s32[512]{0:T(512)S(1)} %bitcast.56, bf16[4096,64]{1,0:T(8,128)(2,1)} %get-tuple-element.147, bf16[8,512,64]{2,1,0:T(8,128)(2,1)} %get-tuple-element.146, s32[]{:T(128)S(6)} %copy.40), kind=kOutput, calls=%fused_computation.2.clone.1 | convolution fusion | flops 276823552 | bytes 9588740 | tf_op jit(solution)/shard_map/while/body/eval_jaxpr/dot_general | solution.py:31
  89.5 3.3 %fusion.44 = bf16[8,512,64]{1,2,0:T(8,128)(2,1)} fusion(bf16[8,512,64]{1,2,0:T(8,128)(2,1)} %get-tuple-element.135, s32[]{:T(128)S(6)} %copy.40, bf16[4096,64]{1,0:T(8,128)(2,1)S(1)} %copy-done.2, f32[512,4096]{1,0:T(8,128)S(1)} %get-tuple-element.124, f32[512]{0:T(512)S(1)} %get-tuple-element.125, s32[4096]{0:T(1024)S(1)} %get-tuple-element.145, ...), kind=kOutput, calls=%fused_computation.9.clone.1 | convolution fusion | flops 281083904 | bytes 9000964 | tf_op jit(solution)/shard_map/while/body/eval_jaxpr/dot_general | solution.py:36
  98.3 3.3 %fusion.44 = bf16[8,512,64]{1,2,0:T(8,128)(2,1)} fusion(bf16[8,512,64]{1,2,0:T(8,128)(2,1)} %get-tuple-element.135, s32[]{:T(128)S(6)} %copy.40, bf16[4096,64]{1,0:T(8,128)(2,1)S(1)} %copy-done.2, f32[512,4096]{1,0:T(8,128)S(1)} %get-tuple-element.124, f32[512]{0:T(512)S(1)} %get-tuple-element.125, s32[4096]{0:T(1024)S(1)} %get-tuple-element.145, ...), kind=kOutput, calls=%fused_computation.9.clone.1 | convolution fusion | flops 281083904 | bytes 9000964 | tf_op jit(solution)/shard_map/while/body/eval_jaxpr/dot_general | solution.py:36
  101.6 2.9 %fusion.42 = (f32[512]{0:T(512)S(1)}, f32[512,4096]{1,0:T(8,128)S(1)}) fusion(s32[4096]{0:T(1024)S(1)} %get-tuple-element.145, s32[512]{0:T(512)S(1)} %bitcast.56, bf16[4096,64]{1,0:T(8,128)(2,1)} %get-tuple-element.147, bf16[8,512,64]{2,1,0:T(8,128)(2,1)} %get-tuple-element.146, s32[]{:T(128)S(6)} %copy.40), kind=kOutput, calls=%fused_computation.2.clone.1 | convolution fusion | flops 276823552 | bytes 9588740 | tf_op jit(solution)/shard_map/while/body/eval_jaxpr/dot_general | solution.py:31
  107.1 3.3 %fusion.44 = bf16[8,512,64]{1,2,0:T(8,128)(2,1)} fusion(bf16[8,512,64]{1,2,0:T(8,128)(2,1)} %get-tuple-element.135, s32[]{:T(128)S(6)} %copy.40, bf16[4096,64]{1,0:T(8,128)(2,1)S(1)} %copy-done.2, f32[512,4096]{1,0:T(8,128)S(1)} %get-tuple-element.124, f32[512]{0:T(512)S(1)} %get-tuple-element.125, s32[4096]{0:T(1024)S(1)} %get-tuple-element.145, ...), kind=kOutput, calls=%fused_computation.9.clone.1 | convolution fusion | flops 281083904 | bytes 9000964 | tf_op jit(solution)/shard_map/while/body/eval_jaxpr/dot_general | solution.py:36
  115.9 3.3 %fusion.44 = bf16[8,512,64]{1,2,0:T(8,128)(2,1)} fusion(bf16[8,512,64]{1,2,0:T(8,128)(2,1)} %get-tuple-element.135, s32[]{:T(128)S(6)} %copy.40, bf16[4096,64]{1,0:T(8,128)(2,1)S(1)} %copy-done.2, f32[512,4096]{1,0:T(8,128)S(1)} %get-tuple-element.124, f32[512]{0:T(512)S(1)} %get-tuple-element.125, s32[4096]{0:T(1024)S(1)} %get-tuple-element.145, ...), kind=kOutput, calls=%fused_computation.9.clone.1 | convolution fusion | flops 281083904 | bytes 9000964 | tf_op jit(solution)/shard_map/while/body/eval_jaxpr/dot_general | solution.py:36
  119.2 2.9 %fusion.42 = (f32[512]{0:T(512)S(1)}, f32[512,4096]{1,0:T(8,128)S(1)}) fusion(s32[4096]{0:T(1024)S(1)} %get-tuple-element.145, s32[512]{0:T(512)S(1)} %bitcast.56, bf16[4096,64]{1,0:T(8,128)(2,1)} %get-tuple-element.147, bf16[8,512,64]{2,1,0:T(8,128)(2,1)} %get-tuple-element.146, s32[]{:T(128)S(6)} %copy.40), kind=kOutput, calls=%fused_computation.2.clone.1 | convolution fusion | flops 276823552 | bytes 9588740 | tf_op jit(solution)/shard_map/while/body/eval_jaxpr/dot_general | solution.py:31
  124.7 3.3 %fusion.44 = bf16[8,512,64]{1,2,0:T(8,128)(2,1)} fusion(bf16[8,512,64]{1,2,0:T(8,128)(2,1)} %get-tuple-element.135, s32[]{:T(128)S(6)} %copy.40, bf16[4096,64]{1,0:T(8,128)(2,1)S(1)} %copy-done.2, f32[512,4096]{1,0:T(8,128)S(1)} %get-tuple-element.124, f32[512]{0:T(512)S(1)} %get-tuple-element.125, s32[4096]{0:T(1024)S(1)} %get-tuple-element.145, ...), kind=kOutput, calls=%fused_computation.9.clone.1 | convolution fusion | flops 281083904 | bytes 9000964 | tf_op jit(solution)/shard_map/while/body/eval_jaxpr/dot_general | solution.py:36
  133.5 3.3 %fusion.44 = bf16[8,512,64]{1,2,0:T(8,128)(2,1)} fusion(bf16[8,512,64]{1,2,0:T(8,128)(2,1)} %get-tuple-element.135, s32[]{:T(128)S(6)} %copy.40, bf16[4096,64]{1,0:T(8,128)(2,1)S(1)} %copy-done.2, f32[512,4096]{1,0:T(8,128)S(1)} %get-tuple-element.124, f32[512]{0:T(512)S(1)} %get-tuple-element.125, s32[4096]{0:T(1024)S(1)} %get-tuple-element.145, ...), kind=kOutput, calls=%fused_computation.9.clone.1 | convolution fusion | flops 281083904 | bytes 9000964 | tf_op jit(solution)/shard_map/while/body/eval_jaxpr/dot_general | solution.py:36
  136.8 2.9 %fusion.42 = (f32[512]{0:T(512)S(1)}, f32[512,4096]{1,0:T(8,128)S(1)}) fusion(s32[4096]{0:T(1024)S(1)} %get-tuple-element.145, s32[512]{0:T(512)S(1)} %bitcast.56, bf16[4096,64]{1,0:T(8,128)(2,1)} %get-tuple-element.147, bf16[8,512,64]{2,1,0:T(8,128)(2,1)} %get-tuple-element.146, s32[]{:T(128)S(6)} %copy.40), kind=kOutput, calls=%fused_computation.2.clone.1 | convolution fusion | flops 276823552 | bytes 9588740 | tf_op jit(solution)/shard_map/while/body/eval_jaxpr/dot_general | solution.py:31
  142.3 3.3 %fusion.44 = bf16[8,512,64]{1,2,0:T(8,128)(2,1)} fusion(bf16[8,512,64]{1,2,0:T(8,128)(2,1)} %get-tuple-element.135, s32[]{:T(128)S(6)} %copy.40, bf16[4096,64]{1,0:T(8,128)(2,1)S(1)} %copy-done.2, f32[512,4096]{1,0:T(8,128)S(1)} %get-tuple-element.124, f32[512]{0:T(512)S(1)} %get-tuple-element.125, s32[4096]{0:T(1024)S(1)} %get-tuple-element.145, ...), kind=kOutput, calls=%fused_computation.9.clone.1 | convolution fusion | flops 281083904 | bytes 9000964 | tf_op jit(solution)/shard_map/while/body/eval_jaxpr/dot_general | solution.py:36
  147.1 3.2 %reshape.71 = bf16[4096,1,64]{2,1,0:T(2,128)(2,1)} reshape(bf16[8,512,64]{2,1,0:T(8,128)(2,1)S(1)} %copy.32) | data formatting | bytes 1048576 | tf_op jit(solution)/shard_map/reshape | solution.py:41
  150.8 23.5 %reduce.1 = bf16[4096,64]{1,0:T(8,128)(2,1)S(1)} reduce(bf16[4096,1,64]{2,1,0:T(2,128)(2,1)} %reshape.71, bf16[]{:T(256)} %broadcast.47), dimensions={1}, to_apply=%reshape.71.reduce_sub_computation | reduce | bytes 1048578 | tf_op jit(solution)/shard_map/reshape | solution.py:41
  175.8 4.1 %all-to-all-start.2 = ((bf16[16,2,8192]{2,1,0:T(2,128)(2,1)}), bf16[16,2,8192]{2,1,0:T(2,128)(2,1)}, u32[]{:S(2)}, u32[]{:S(2)}) async-start(bf16[16,2,8192]{2,1,0:T(2,128)(2,1)} %reshape.73), calls=%async_computation.2 | async-start | bytes 1048576 | tf_op jit(solution)/shard_map/all_to_all | solution.py:42
  182.6 14.7 %all-to-all-done.2 = bf16[16,2,8192]{2,1,0:T(2,128)(2,1)} async-done(((bf16[16,2,8192]{2,1,0:T(2,128)(2,1)}), bf16[16,2,8192]{2,1,0:T(2,128)(2,1)}, u32[]{:S(2)}, u32[]{:S(2)}) %all-to-all-start.2) | async-done | bytes 524320 | tf_op jit(solution)/shard_map/all_to_all | solution.py:42
  197.2 5.5 %reshape.74 = bf16[4096,1,64]{2,1,0:T(2,128)(2,1)} reshape(bf16[16,2,8192]{2,1,0:T(2,128)(2,1)} %all-to-all-done.2) | data formatting | bytes 1048576
  202.8 4.6 %copy.28 = bf16[4096,1,64]{0,2,1:T(8,128)(2,1)S(1)} copy(bf16[4096,1,64]{2,1,0:T(2,128)(2,1)} %reshape.74) | data formatting | bytes 1048576 | tf_op jit(solution)/shard_map/all_to_all | solution.py:42
  (68 shorter events, 52.1 us)
Async XLA Ops:
  0.6 207.0 %copy-start = (bf16[1024,1024]{1,0:T(8,128)(2,1)S(1)}, bf16[1024,1024]{1,0:T(8,128)(2,1)}, u32[]{:S(2)}) copy-start(bf16[1024,1024]{1,0:T(8,128)(2,1)} %param.12) | copy-start | bytes 6291460
  2.1 18.5 %all-to-all-start = ((s32[16,256,1]{1,2,0:T(1,128)}), s32[16,256,1]{1,2,0:T(1,128)S(1)}, u32[]{:S(2)}, u32[]{:S(2)}) async-start(s32[16,256,1]{1,2,0:T(1,128)} %concatenate.4), calls=%async_computation | async-start | bytes 32768 | tf_op jit(solution)/shard_map/all_to_all | solution.py:16
  20.6 45.9 %all-to-all-start.1 = ((bf16[256,16,192]{0,2,1:T(8,128)(2,1)}), bf16[256,16,192]{0,2,1:T(8,128)(2,1)}, u32[]{:S(2)}, u32[]{:S(2)}) async-start(bf16[256,16,192]{0,2,1:T(8,128)(2,1)} %bitcast.50), calls=%async_computation.1 | async-start | bytes 3145728 | tf_op jit(solution)/shard_map/all_to_all | solution.py:19
  68.0 1.2 copy-start.1
  75.2 5.5 %copy-start.2 = (bf16[4096,64]{1,0:T(8,128)(2,1)S(1)}, bf16[4096,64]{1,0:T(8,128)(2,1)}, u32[]{:S(2)}) copy-start(bf16[4096,64]{1,0:T(8,128)(2,1)} %get-tuple-element.148) | copy-start | bytes 1572868 | tf_op jit(solution)/shard_map/while
  84.0 5.5 %copy-start.2 = (bf16[4096,64]{1,0:T(8,128)(2,1)S(1)}, bf16[4096,64]{1,0:T(8,128)(2,1)}, u32[]{:S(2)}) copy-start(bf16[4096,64]{1,0:T(8,128)(2,1)} %get-tuple-element.148) | copy-start | bytes 1572868 | tf_op jit(solution)/shard_map/while
  92.8 5.5 %copy-start.2 = (bf16[4096,64]{1,0:T(8,128)(2,1)S(1)}, bf16[4096,64]{1,0:T(8,128)(2,1)}, u32[]{:S(2)}) copy-start(bf16[4096,64]{1,0:T(8,128)(2,1)} %get-tuple-element.148) | copy-start | bytes 1572868 | tf_op jit(solution)/shard_map/while
  101.6 5.5 %copy-start.2 = (bf16[4096,64]{1,0:T(8,128)(2,1)S(1)}, bf16[4096,64]{1,0:T(8,128)(2,1)}, u32[]{:S(2)}) copy-start(bf16[4096,64]{1,0:T(8,128)(2,1)} %get-tuple-element.148) | copy-start | bytes 1572868 | tf_op jit(solution)/shard_map/while
  110.4 5.5 %copy-start.2 = (bf16[4096,64]{1,0:T(8,128)(2,1)S(1)}, bf16[4096,64]{1,0:T(8,128)(2,1)}, u32[]{:S(2)}) copy-start(bf16[4096,64]{1,0:T(8,128)(2,1)} %get-tuple-element.148) | copy-start | bytes 1572868 | tf_op jit(solution)/shard_map/while
  119.2 5.5 %copy-start.2 = (bf16[4096,64]{1,0:T(8,128)(2,1)S(1)}, bf16[4096,64]{1,0:T(8,128)(2,1)}, u32[]{:S(2)}) copy-start(bf16[4096,64]{1,0:T(8,128)(2,1)} %get-tuple-element.148) | copy-start | bytes 1572868 | tf_op jit(solution)/shard_map/while
  128.0 5.5 %copy-start.2 = (bf16[4096,64]{1,0:T(8,128)(2,1)S(1)}, bf16[4096,64]{1,0:T(8,128)(2,1)}, u32[]{:S(2)}) copy-start(bf16[4096,64]{1,0:T(8,128)(2,1)} %get-tuple-element.148) | copy-start | bytes 1572868 | tf_op jit(solution)/shard_map/while
  136.8 5.5 %copy-start.2 = (bf16[4096,64]{1,0:T(8,128)(2,1)S(1)}, bf16[4096,64]{1,0:T(8,128)(2,1)}, u32[]{:S(2)}) copy-start(bf16[4096,64]{1,0:T(8,128)(2,1)} %get-tuple-element.148) | copy-start | bytes 1572868 | tf_op jit(solution)/shard_map/while
  150.8 56.9 %copy-start.3 = (f32[1024]{0:T(1024)S(1)}, f32[1024]{0:T(1024)}, u32[]{:S(2)}) copy-start(f32[1024]{0:T(1024)} %param.13) | copy-start | bytes 12292
  175.8 21.4 %all-to-all-start.2 = ((bf16[16,2,8192]{2,1,0:T(2,128)(2,1)}), bf16[16,2,8192]{2,1,0:T(2,128)(2,1)}, u32[]{:S(2)}, u32[]{:S(2)}) async-start(bf16[16,2,8192]{2,1,0:T(2,128)(2,1)} %reshape.73), calls=%async_computation.2 | async-start | bytes 1048576 | tf_op jit(solution)/shard_map/all_to_all | solution.py:42
  179.9 29.9 %copy-start.4 = (f32[1024]{0:T(1024)S(1)}, f32[1024]{0:T(1024)}, u32[]{:S(2)}) copy-start(f32[1024]{0:T(1024)} %param.15) | copy-start | bytes 12292
  179.9 29.9 %copy-start.5 = (f32[1024]{0:T(1024)S(1)}, f32[1024]{0:T(1024)}, u32[]{:S(2)}) copy-start(f32[1024]{0:T(1024)} %param.14) | copy-start | bytes 12292
